TPU v7x, 32 devices: a whole 2x2x4 slice. The times are simulated.
32 devices in a mesh: grp: 2 (over x), ma: 16 (over z, y, core).
Axes of the slice: x: 2, y: 2, z: 4, core: 2. Of those that a mesh axis runs over, the one named last changes fastest.
Arguments:
- vis: float32 [16384, 2, 256], P(('grp', 'ma')), parts along dimension 0, may hold values from -6 to 6
- transfer: bfloat16 [32, 2, 256, 1024], P(('grp', 'ma')), parts along dimension 0, may hold values from -0.1875 to 0.1875
- band_start: int32 [2], P('grp'), parts along dimension 0, may hold values from 0 to 8176
- comp_index: int32 [2048], P(('grp', 'ma')), parts along dimension 0, may hold values from 0 to 16383
- comp_amp: int32 [2048, 2], P(('grp', 'ma')), parts along dimension 0, may hold values from -4096 to 4096
Outputs:
- residual_alm: float32 [32, 2, 1024], P(('grp', 'ma')), parts along dimension 0
There are 2 independent parts, one for each index of `grp`. A program takes and returns all parts, laid end to end along the dimension named above; each array names one. Nothing has to cross between parts.
All inputs are finite; a program needn't handle non-finite values.
Results may differ from a plain program's by a relative error of at most 0.003.
Values sent between devices are 32-bit elements; how exact they have to be, the bound alone decides.
No kernel may reach another device: no remote copies, remote signals or barrier semaphores. Data moves between devices by JAX's collectives and lax.ppermute only.
A program may use at most 64 MiB of HBM per device.

v0:
```python
import math
import jax
import jax.numpy as jnp
from jax import lax
from jax.sharding import PartitionSpec as P

SIDEREAL_TICKS = 8192


def trig_pair_lookup(azimuthal_orders, tick_moments):
    rotation_radians = azimuthal_orders[:, None] * tick_moments[None, :] % SIDEREAL_TICKS
    angle = rotation_radians.astype(jnp.float32) * (2.0 * math.pi / SIDEREAL_TICKS)
    return jnp.concatenate([jnp.cos(angle), jnp.sin(angle)], 0)


def combine_parts(product, row_count):
    product = product.reshape(2, row_count, 2, -1)
    scale = 1.0 / math.sqrt(SIDEREAL_TICKS)
    real_part = (product[0, :, 0] + product[1, :, 1]) * scale
    imag_part = (product[0, :, 1] - product[1, :, 0]) * scale
    return jnp.stack([real_part, imag_part], 1)


def body(vis, transfer, band_start, comp_index, comp_amp):
    ma_count = lax.axis_size("ma")
    device_rank = lax.axis_index("ma")
    m_local = transfer.shape[0]
    width = transfer.shape[3]
    modes = m_local * ma_count
    regrouped = lax.all_to_all(vis, "ma", split_axis=2, concat_axis=0, tiled=True)
    azimuthal_orders = band_start[0] + jnp.arange(modes, dtype=jnp.int32)
    trig_pair = trig_pair_lookup(azimuthal_orders, jnp.arange(SIDEREAL_TICKS, dtype=jnp.int32))
    flat_visibility = regrouped.reshape(SIDEREAL_TICKS, -1)
    product = jnp.dot(
        trig_pair,
        flat_visibility,
        precision=lax.Precision.HIGHEST,
        preferred_element_type=jnp.float32,
    )
    local_spectra = combine_parts(product, modes)
    spectra = lax.all_to_all(local_spectra, "ma", split_axis=0, concat_axis=2, tiled=True)
    index_all, amp_all = (
        lax.all_gather(comp_index, "ma", axis=0, tiled=True),
        lax.all_gather(comp_amp, "ma", axis=0, tiled=True),
    )
    slots = m_local * width
    offset = index_all - device_rank * slots
    inside = (offset >= 0) & (offset < slots)
    target = jnp.where(inside, offset, slots)
    summed = jax.ops.segment_sum(amp_all, target, num_segments=slots + 1)[:slots]
    model_alm = (
        (summed.astype(jnp.float32) * (1.0 / 1024.0))
        .astype(jnp.bfloat16)
        .reshape(m_local, width, 2)
    )
    predicted = jnp.einsum(
        "mcbl,mlk->mcbk", transfer, model_alm, preferred_element_type=jnp.float32
    )
    pred_real = predicted[:, 0, :, 0] - predicted[:, 1, :, 1]
    pred_imag = predicted[:, 0, :, 1] + predicted[:, 1, :, 0]
    resid_vis = (spectra - jnp.stack([pred_real, pred_imag], 1)).astype(jnp.bfloat16)
    projected = jnp.einsum(
        "mcbl,mkb->mkcl", transfer, resid_vis, preferred_element_type=jnp.float32
    )
    alm_real = projected[:, 0, 0] + projected[:, 1, 1]
    alm_imag = projected[:, 1, 0] - projected[:, 0, 1]
    return jnp.stack([alm_real, alm_imag], 1)


def solution(mesh):
    in_specs = (
        P(("grp", "ma"), None, None),
        P(("grp", "ma"), None, None, None),
        P("grp"),
        P(("grp", "ma")),
        P(("grp", "ma"), None),
    )
    out_specs = P(("grp", "ma"), None, None)
    return jax.shard_map(body, mesh=mesh, in_specs=in_specs, out_specs=out_specs, check_vma=False)
```

profile of v0, /device:TPU:0, one launch (start us, length us, event | category | flops | bytes accessed | tf_op | source)
XLA Modules:
  0.0 85.9 jit_solution(13697554280180083877)
XLA Ops:
  0.0 0.0 copy-start
  0.0 3.7 %copy.34 = f32[512,2,256]{0,1,2:T(2,128)} copy(f32[512,2,256]{2,1,0:T(2,128)} %param.5) | data formatting | bytes 2097152 | tf_op args[0]
  3.7 7.4 %all-to-all-start = ((f32[512,2,256]{0,1,2:T(2,128)}), f32[512,2,256]{0,1,2:T(2,128)S(1)}, u32[]{:S(2)}, u32[]{:S(2)}) async-start(f32[512,2,256]{0,1,2:T(2,128)} %copy.34), calls=%async_computation | async-start | bytes 2097152 | tf_op jit(solution)/shard_map/all_to_all | solution.py:30
  11.8 0.0 copy-start.3
  11.8 0.6 copy-done.3
  12.5 0.6 dynamic-slice
  13.7 0.0 copy-start.2
  13.7 0.6 copy-done.2
  14.4 0.2 dynamic-update-slice
  14.5 23.3 %all-reduce = s32[1024]{0:T(1024)S(1)} all-reduce(s32[1024]{0:T(1024)S(1)} %dynamic-update-slice), channel_id=1, replica_groups=mesh['grp'=2,'ma'=16] {'ma'}, use_global_device_ids=true, to_apply=%add | all-reduce | flops 1024 | bytes 8192
  37.8 0.7 copy-done.1
  38.5 19.5 %all-gather = s32[16,64,2]{1,2,0:T(2,128)S(1)} all-gather(s32[1,64,2]{1,2,0:T(2,128)S(1)} %bitcast.60), channel_id=1, replica_groups=mesh['grp'=2,'ma'=16] {'ma'}, dimensions={0}, use_global_device_ids=true | all-gather | bytes 8704 | tf_op jit(solution)/shard_map/all_gather | solution.py:44
  58.0 0.2 copy.43
  58.2 7.4 %scatter_custom_fusion = s32[1025,2]{1,0:T(8,128)S(1)} fusion(s32[1024]{0:T(1024)S(1)} %and_select_fusion, s32[1024,2]{1,0:T(8,128)S(1)} %bitcast.59, s32[]{:T(128)} %constant.9.clone.1), kind=kCustom, calls=%fused_computation.16 | custom fusion | flops 2048 | bytes 8204 | tf_op jit(solution)/shard_map/scatter-add | solution.py:50
  65.7 0.1 multiply_convert_fusion
  65.7 0.1 copy.47
  65.9 0.4 convolution_bitcast_fusion.1
  66.2 2.1 %fusion.11 = (f32[16,8192]{1,0:T(8,128)S(1)}, f32[16,8192]{1,0:T(8,128)S(1)}) fusion(s32[16]{0:T(128)S(1)} %iota_add_fusion), kind=kLoop, calls=%fused_computation.19 | loop fusion | flops 1835008 | bytes 1048640 | tf_op jit(solution)/shard_map/cos | solution.py:13
  68.4 0.1 pad_maximum_fusion
  68.5 0.0 all-to-all-done
  68.5 0.2 copy.35
  68.7 0.6 copy.36
  69.3 0.6 copy.46
  69.9 4.4 %fusion.22 = f32[2,16,2,16]{3,1,2,0:T(8,128)S(1)} fusion(f32[2,16,8192,1]{2,1,3,0:T(8,128)S(1)} %bitcast.55, f32[2,16,8192,1]{2,1,0,3:T(8,128)S(1)} %bitcast.56), kind=kOutput, calls=%fused_computation.41 | convolution fusion | flops 100663296 | bytes 2101248 | tf_op jit(solution)/shard_map/dot_general | solution.py:34
  74.4 0.6 copy.37
  75.0 3.5 %all-to-all-start.1 = ((f32[16,2,16]{2,1,0:T(2,128)}), f32[16,2,16]{2,1,0:T(2,128)S(1)}, u32[]{:S(2)}, u32[]{:S(2)}) async-start(f32[16,2,16]{2,1,0:T(2,128)} %copy.37), calls=%async_computation.1 | async-start | bytes 32768 | tf_op jit(solution)/shard_map/all_to_all | solution.py:41
  78.5 0.1 add.66
  78.6 0.1 sub.60
  78.6 6.3 %all-to-all-done.1 = f32[16,2,16]{2,1,0:T(2,128)S(1)} async-done(((f32[16,2,16]{2,1,0:T(2,128)}), f32[16,2,16]{2,1,0:T(2,128)S(1)}, u32[]{:S(2)}, u32[]{:S(2)}) %all-to-all-start.1) | async-done | bytes 2080 | tf_op jit(solution)/shard_map/all_to_all | solution.py:41
  84.9 0.1 reshape.206
  85.0 0.2 convolution_bitcast_fusion
  85.3 0.6 pad_maximum_fusion.2
  (10 shorter events, 0.1 us)
Async XLA Ops:
  0.0 65.9 %copy-start = (bf16[1,2,256,1024]{3,2,1,0:T(8,128)(2,1)S(1)}, bf16[1,2,256,1024]{3,2,1,0:T(8,128)(2,1)}, u32[]{:S(2)}) copy-start(bf16[1,2,256,1024]{3,2,1,0:T(8,128)(2,1)} %param.6) | copy-start | bytes 3145732
  3.7 64.7 %all-to-all-start = ((f32[512,2,256]{0,1,2:T(2,128)}), f32[512,2,256]{0,1,2:T(2,128)S(1)}, u32[]{:S(2)}, u32[]{:S(2)}) async-start(f32[512,2,256]{0,1,2:T(2,128)} %copy.34), calls=%async_computation | async-start | bytes 2097152 | tf_op jit(solution)/shard_map/all_to_all | solution.py:30
  11.8 0.7 copy-start.3
  13.7 0.7 copy-start.2
  37.8 0.7 copy-start.1
  75.0 9.9 %all-to-all-start.1 = ((f32[16,2,16]{2,1,0:T(2,128)}), f32[16,2,16]{2,1,0:T(2,128)S(1)}, u32[]{:S(2)}, u32[]{:S(2)}) async-start(f32[16,2,16]{2,1,0:T(2,128)} %copy.37), calls=%async_computation.1 | async-start | bytes 32768 | tf_op jit(solution)/shard_map/all_to_all | solution.py:41
where the time goes:
time: 86.3 us; the launch traced here: 85.9 us
  blocking collectives  42.8 us (50%)
  starting transfers between devices  10.9 us (13%)
  other arithmetic  10.3 us (12%)
  local copies, waits for them, and re-layouts  9.1 us (11%)
  waiting for transfers between devices  6.29 us (7%)
  matrix products  5.05 us (6%)
  between operations  1.48 us (2%)
    unnamed x1, blocking collectives  23.3 us
    all_gather x1, blocking collectives, body(): lax.all_gather(comp_amp, 'ma', axis=0, tiled=True)  19.5 us
    unnamed x15, local copies, waits for them, and re-layouts  7.42 us
    all_to_all x1, starting transfers between devices, body(): lax.all_to_all(vis, 'ma', split_axis=2, concat_axis=0, tiled=True)  7.41 us
    scatter-add x1, other arithmetic, body(): jax.ops.segment_sum(amp_all, target, num_segments=slots + 1)[:slots]  7.41 us
    all_to_all x1, waiting for transfers between devices, body(): lax.all_to_all(local_spectra, 'ma', split_axis=0, concat_axis=2, tiled=True)  6.28 us
    dot_general x1, matrix products, body(): jnp.dot(trig_pair, flat_visibility, precision=lax.Precision.HIGHEST, pref...  4.42 us
    all_to_all x1, starting transfers between devices, body(): lax.all_to_all(local_spectra, 'ma', split_axis=0, concat_axis=2, tiled=True)  3.47 us
  transfers between devices with their start and end apart: 2, of which 1 were waited for; matrix products, arithmetic and copies ran while one was open for 13% of the time, Pallas kernels for 0%

commit v1 on v0

--- a/solution.py
+++ b/solution.py
@@ -41,7 +41,9 @@
     spectra = lax.all_to_all(local_spectra, "ma", split_axis=0, concat_axis=2, tiled=True)
     index_all, amp_all = (
         lax.all_gather(comp_index, "ma", axis=0, tiled=True),
-        lax.all_gather(comp_amp, "ma", axis=0, tiled=True),
+        jnp.concatenate(
+            lax.all_to_all(jnp.stack([comp_amp] * lax.axis_size("ma")), "ma", 0, 0), axis=0
+        ),
     )
     slots = m_local * width
     offset = index_all - device_rank * slots

time: 86.3 us -> 77.7 us (0.900)
  blocking collectives: 42.8 us -> 20.7 us
  other arithmetic: 10.3 us -> 15.5 us
  starting transfers between devices: 10.9 us -> 14.9 us
  waiting for transfers between devices: 6.29 us -> 8.41 us
  local copies, waits for them, and re-layouts: 9.1 us -> 11.2 us
    all_gather x1 -> x0, blocking collectives: 19.5 us -> none  [body(): lax.all_gather(comp_amp, 'ma', axis=0, tiled=True)]
    all_to_all x0 -> x1, starting transfers between devices: none -> 7.41 us  [body(): lax.all_to_all(jnp.stack([comp_amp] * lax.axis_size('ma')), 'ma', 0, 0)]
    all_to_all x1, starting transfers between devices: 7.41 us -> 3.94 us  [body(): lax.all_to_all(vis, 'ma', split_axis=2, concat_axis=0, tiled=True)]
    unnamed x1, blocking collectives: 23.3 us -> 20.7 us
    all_to_all x0 -> x1, waiting for transfers between devices: none -> 2.08 us  [body(): lax.all_to_all(jnp.stack([comp_amp] * lax.axis_size('ma')), 'ma', 0, 0)]
    concatenate x1, other arithmetic: 0.07 us -> 1.27 us  [trig_pair_lookup(): return jnp.concatenate([jnp.cos(angle), jnp.sin(angle)], 0)]
    cos x1, other arithmetic: 2.13 us -> 3.26 us  [trig_pair_lookup(): return jnp.concatenate([jnp.cos(angle), jnp.sin(angle)], 0)]
    scatter-add x1, other arithmetic: 7.41 us -> 8.52 us  [body(): jax.ops.segment_sum(amp_all, target, num_segments=slots + 1)[:slots]]
  transfers between devices with their start and end apart: 2 -> 3, of which waited for: 1 -> 2; matrix products, arithmetic and copies ran while one was open for 13% -> 28% of each run, Pallas kernels for 0% -> 0%
where the time goes in v1:
time: 77.7 us; the launch traced here: 77.2 us
  blocking collectives  20.7 us (27%)
  other arithmetic  15.5 us (20%)
  starting transfers between devices  14.9 us (19%)
  local copies, waits for them, and re-layouts  11.2 us (14%)
  waiting for transfers between devices  8.41 us (11%)
  matrix products  5.05 us (6%)
  between operations  1.43 us (2%)
    unnamed x1, blocking collectives  20.7 us
    scatter-add x1, other arithmetic, body(): jax.ops.segment_sum(amp_all, target, num_segments=slots + 1)[:slots]  8.52 us
    unnamed x15, local copies, waits for them, and re-layouts  7.96 us
    all_to_all x1, starting transfers between devices, body(): lax.all_to_all(jnp.stack([comp_amp] * lax.axis_size('ma')), 'ma', 0, 0)  7.41 us
    all_to_all x1, waiting for transfers between devices, body(): lax.all_to_all(local_spectra, 'ma', split_axis=0, concat_axis=2, tiled=True)  6.32 us
    dot_general x1, matrix products, body(): jnp.dot(trig_pair, flat_visibility, precision=lax.Precision.HIGHEST, pref...  4.42 us
    all_to_all x1, starting transfers between devices, body(): lax.all_to_all(vis, 'ma', split_axis=2, concat_axis=0, tiled=True)  3.94 us
    all_to_all x1, starting transfers between devices, body(): lax.all_to_all(local_spectra, 'ma', split_axis=0, concat_axis=2, tiled=True)  3.58 us
  transfers between devices with their start and end apart: 3, of which 2 were waited for; matrix products, arithmetic and copies ran while one was open for 28% of the time, Pallas kernels for 0%

profile of v1, /device:TPU:0, one launch (start us, length us, event | category | flops | bytes accessed | tf_op | source)
XLA Modules:
  0.0 77.2 jit_solution(13121800190383370915)
XLA Ops:
  0.0 0.8 broadcast_bitcast_fusion
  0.8 0.7 reshape.226
  1.5 7.4 %all-to-all-start.2 = ((s32[16,1,128]{2,1,0:T(1,128)}), s32[16,1,128]{2,1,0:T(1,128)S(1)}, u32[]{:S(2)}, u32[]{:S(2)}) async-start(s32[16,1,128]{2,1,0:T(1,128)} %reshape.226), calls=%async_computation.2 | async-start | bytes 16384 | tf_op jit(solution)/shard_map/all_to_all | solution.py:45
  9.5 3.6 %copy.31 = f32[512,2,256]{0,1,2:T(2,128)} copy(f32[512,2,256]{2,1,0:T(2,128)} %param.5) | data formatting | bytes 2097152 | tf_op args[0]
  13.2 2.1 %all-to-all-done.2 = s32[16,1,128]{2,1,0:T(1,128)S(1)} async-done(((s32[16,1,128]{2,1,0:T(1,128)}), s32[16,1,128]{2,1,0:T(1,128)S(1)}, u32[]{:S(2)}, u32[]{:S(2)}) %all-to-all-start.2) | async-done | bytes 8224 | tf_op jit(solution)/shard_map/all_to_all | solution.py:45
  15.2 3.9 %all-to-all-start = ((f32[512,2,256]{0,1,2:T(2,128)}), f32[512,2,256]{0,1,2:T(2,128)S(1)}, u32[]{:S(2)}, u32[]{:S(2)}) async-start(f32[512,2,256]{0,1,2:T(2,128)} %copy.31), calls=%async_computation | async-start | bytes 2097152 | tf_op jit(solution)/shard_map/all_to_all | solution.py:30
  19.2 3.3 %fusion.11 = (f32[16,8192]{1,0:T(8,128)}, f32[16,8192]{1,0:T(8,128)}) fusion(s32[16]{0:T(128)S(1)} %iota_add_fusion), kind=kLoop, calls=%fused_computation.19 | loop fusion | flops 1835008 | bytes 1048640 | tf_op jit(solution)/shard_map/cos | solution.py:13
  22.5 0.7 copy-done.2
  23.1 0.6 dynamic-slice
  24.4 0.6 copy-done.1
  25.0 0.2 dynamic-update-slice
  25.2 20.7 %all-reduce = s32[1024]{0:T(1024)S(1)} all-reduce(s32[1024]{0:T(1024)S(1)} %dynamic-update-slice), channel_id=1, replica_groups=mesh['grp'=2,'ma'=16] {'ma'}, use_global_device_ids=true, to_apply=%add | all-reduce | flops 1024 | bytes 8192
  45.9 1.3 %pad_maximum_fusion = f32[32,8192]{1,0:T(8,128)S(1)} fusion(f32[16,8192]{1,0:T(8,128)} %get-tuple-element.12, f32[16,8192]{1,0:T(8,128)} %get-tuple-element.11), kind=kLoop, calls=%fused_computation.3 | loop fusion | flops 262144 | bytes 2097152 | tf_op jit(solution)/shard_map/concatenate | solution.py:13
  47.2 0.5 broadcast.51
  47.7 0.7 reduce.8
  48.4 0.1 reshape.227
  48.4 1.1 %copy.40 = s32[16,64,2]{2,1,0:T(8,128)} copy(s32[16,64,2]{1,2,0:T(2,128)S(1)} %bitcast.62) | data formatting | bytes 16384 | tf_op jit(solution)/shard_map/reshape | solution.py:44
  49.5 8.5 %scatter_custom_fusion = s32[1025,2]{1,0:T(8,128)} fusion(s32[1024]{0:T(1024)S(1)} %and_select_fusion, s32[1024,2]{1,0:T(8,128)} %bitcast.61, s32[]{:T(128)} %constant.9.clone.1), kind=kCustom, calls=%fused_computation.16 | custom fusion | flops 2048 | bytes 8712 | tf_op jit(solution)/shard_map/scatter-add | solution.py:52
  58.0 1.1 %multiply_convert_fusion = bf16[1024,2]{1,0:T(8,128)(2,1)S(1)} fusion(s32[1025,2]{1,0:T(8,128)} %scatter_custom_fusion), kind=kLoop, calls=%fused_computation.12 | loop fusion | flops 6144 | bytes 12288 | tf_op jit(solution)/shard_map/convert_element_type | solution.py:55
  59.1 0.1 copy.44
  59.3 0.4 convolution_bitcast_fusion.1
  59.6 0.2 copy.32
  59.9 0.6 copy.33
  60.5 0.6 copy.43
  61.1 4.4 %fusion.22 = f32[2,16,2,16]{3,1,2,0:T(8,128)S(1)} fusion(f32[2,16,8192,1]{2,1,3,0:T(8,128)S(1)} %bitcast.57, f32[2,16,8192,1]{2,1,0,3:T(8,128)S(1)} %bitcast.58), kind=kOutput, calls=%fused_computation.42 | convolution fusion | flops 100663296 | bytes 2101248 | tf_op jit(solution)/shard_map/dot_general | solution.py:34
  65.6 0.6 copy.34
  66.2 3.6 %all-to-all-start.1 = ((f32[16,2,16]{2,1,0:T(2,128)}), f32[16,2,16]{2,1,0:T(2,128)S(1)}, u32[]{:S(2)}, u32[]{:S(2)}) async-start(f32[16,2,16]{2,1,0:T(2,128)} %copy.34), calls=%async_computation.1 | async-start | bytes 32768 | tf_op jit(solution)/shard_map/all_to_all | solution.py:41
  69.8 0.1 add.66
  69.9 6.3 %all-to-all-done.1 = f32[16,2,16]{2,1,0:T(2,128)S(1)} async-done(((f32[16,2,16]{2,1,0:T(2,128)}), f32[16,2,16]{2,1,0:T(2,128)S(1)}, u32[]{:S(2)}, u32[]{:S(2)}) %all-to-all-start.1) | async-done | bytes 2080 | tf_op jit(solution)/shard_map/all_to_all | solution.py:41
  76.3 0.1 reshape.210
  76.4 0.2 convolution_bitcast_fusion
  76.6 0.6 pad_maximum_fusion.2
  (14 shorter events, 0.2 us)
Async XLA Ops:
  0.0 59.3 %copy-start = (bf16[1,2,256,1024]{3,2,1,0:T(8,128)(2,1)S(1)}, bf16[1,2,256,1024]{3,2,1,0:T(8,128)(2,1)}, u32[]{:S(2)}) copy-start(bf16[1,2,256,1024]{3,2,1,0:T(8,128)(2,1)} %param.6) | copy-start | bytes 3145732
  1.5 13.8 %all-to-all-start.2 = ((s32[16,1,128]{2,1,0:T(1,128)}), s32[16,1,128]{2,1,0:T(1,128)S(1)}, u32[]{:S(2)}, u32[]{:S(2)}) async-start(s32[16,1,128]{2,1,0:T(1,128)} %reshape.226), calls=%async_computation.2 | async-start | bytes 16384 | tf_op jit(solution)/shard_map/all_to_all | solution.py:45
  15.2 44.4 %all-to-all-start = ((f32[512,2,256]{0,1,2:T(2,128)}), f32[512,2,256]{0,1,2:T(2,128)S(1)}, u32[]{:S(2)}, u32[]{:S(2)}) async-start(f32[512,2,256]{0,1,2:T(2,128)} %copy.31), calls=%async_computation | async-start | bytes 2097152 | tf_op jit(solution)/shard_map/all_to_all | solution.py:30
  22.5 0.7 copy-start.2
  24.3 0.7 copy-start.1
  66.2 10.1 %all-to-all-start.1 = ((f32[16,2,16]{2,1,0:T(2,128)}), f32[16,2,16]{2,1,0:T(2,128)S(1)}, u32[]{:S(2)}, u32[]{:S(2)}) async-start(f32[16,2,16]{2,1,0:T(2,128)} %copy.34), calls=%async_computation.1 | async-start | bytes 32768 | tf_op jit(solution)/shard_map/all_to_all | solution.py:41
